TPU v7x, 32 devices: a whole 2x2x4 slice. The times are simulated.
32 devices in a mesh: chan: 8 (over z, x), grp: 4 (over y, core).
Axes of the slice: x: 2, y: 2, z: 4, core: 2. Of those that a mesh axis runs over, the one named last changes fastest.
Arguments:
- voltage_real: bfloat16 [512, 4, 2, 256, 128], P('chan', 'grp'), may hold values from -6 to 6
- voltage_imag: bfloat16 [512, 4, 2, 256, 128], P('chan', 'grp'), may hold values from -6 to 6
- gain_real: float32 [512, 4, 2, 256], P('chan', 'grp'), may hold values from -3 to 3
- gain_imag: float32 [512, 4, 2, 256], P('chan', 'grp'), may hold values from -3 to 3
- channel_mask: int32 [8192], replicated, may hold values 0 or 1
- beam_owner: int32 [4, 256], P('grp'), may hold values from 0 to 255, each once within a row
Outputs:
- flagged: bfloat16 [2, 1024, 65536], P(None, ('chan', 'grp'))
- common_mode: float32 [65536], P(('chan', 'grp'))
Inputs may be any that keep to these rules, and one draw needn't show every extreme that they name: Each row of beam_owner names every number of 0 to 255 once.
All inputs are finite; a program needn't handle non-finite values.
Results may differ from a plain program's by a relative error of at most 0.0015.
The roundings to bfloat16 on the way count: a program that leaves them out, or rounds other values in their place, can miss the bound.
Values may be sent and summed in bfloat16 or wider, within the bound.
No kernel may reach another device: no remote copies, remote signals or barrier semaphores. Data moves between devices by JAX's collectives and lax.ppermute only.
A program may use at most 256 MiB of HBM per device.

v0:
```python
import math
import jax
import jax.numpy as jnp
from jax import lax
from jax.sharding import PartitionSpec as P

FEEDS_NS = 256
CYL = 4
UP = 16
epsilon = 1e-05


def beam_table(feed_count):
    counter = jnp.arange(feed_count, dtype=jnp.int32)
    phases = counter[:, None] * counter[None, :] % feed_count
    angles = phases.astype(jnp.float32) * (-2.0 * math.pi / feed_count)
    factor = 1.0 / math.sqrt(feed_count)
    cosine = jnp.cos(angles) * factor
    sines = jnp.sin(angles) * factor
    real_rows = jnp.stack([cosine, -sines], axis=1)
    imaginary_rows = jnp.stack([sines, cosine], axis=1)
    return jnp.stack([real_rows, imaginary_rows], axis=0).astype(jnp.bfloat16)


def stokes_table(column_count, up_count):
    columns = jnp.arange(column_count, dtype=jnp.int32)
    spectral = jnp.arange(up_count, dtype=jnp.int32)
    column_phase = columns[:, None] * columns[None, :] % column_count
    spectral_phase = spectral[:, None] * spectral[None, :] % up_count
    phases = (
        column_phase[:, None, :, None] * up_count + spectral_phase[None, :, None, :] * column_count
    )
    angles = phases.astype(jnp.float32) * (-2.0 * math.pi / (column_count * up_count))
    factor = 1.0 / math.sqrt(column_count * up_count)
    cosine = jnp.cos(angles) * factor
    sines = jnp.sin(angles) * factor
    real_rows = jnp.stack([cosine, -sines], axis=2)
    imaginary_rows = jnp.stack([sines, cosine], axis=2)
    return jnp.stack([real_rows, imaginary_rows], axis=0)


def calibrate(voltage_real, voltage_imag, gain_real, gain_imag):
    real_gain = gain_real[..., None]
    imaginary_gain = gain_imag[..., None]
    real_volt = voltage_real.astype(jnp.float32)
    imaginary_volt = voltage_imag.astype(jnp.float32)
    real_part = real_gain * real_volt - imaginary_gain * imaginary_volt
    imaginary_part = real_gain * imaginary_volt + imaginary_gain * real_volt
    return jnp.stack([real_part, imaginary_part], axis=-3).astype(jnp.bfloat16)


def beamform(calibrated, weights):
    formed = jnp.einsum(
        "amrn,cyprns->cypams", weights, calibrated, preferred_element_type=jnp.float32
    )
    return formed.astype(jnp.bfloat16)


def detect_block(formed, weights):
    channel_count, column_count, pol_count, parts_count, beam_count, sample_count = formed.shape
    up_count = weights.shape[2]
    frame_count = sample_count // up_count
    shaped = formed.reshape(
        channel_count, column_count, pol_count, parts_count, beam_count, frame_count, up_count
    ).astype(jnp.float32)
    fields = jnp.einsum("aekrqu,cqprmfu->cpaemkf", weights, shaped, precision=lax.Precision.HIGHEST)
    first_real = fields[:, 0, 0]
    first_imaginary = fields[:, 0, 1]
    second_real = fields[:, 1, 0]
    second_imaginary = fields[:, 1, 1]
    intensity = (
        first_real * first_real
        + first_imaginary * first_imaginary
        + second_real * second_real
        + second_imaginary * second_imaginary
    )
    circular = 2.0 * (first_imaginary * second_real - first_real * second_imaginary)
    stacked = jnp.stack([intensity, circular], axis=1).reshape(
        channel_count, 2, weights.shape[1], beam_count, sample_count
    )
    return stacked.astype(jnp.bfloat16)


def soft_flag(spectra, common, mask_grid):
    coarse_count, stokes_count, beam_count, sample_count = spectra.shape
    up_count = mask_grid.shape[1]
    frame_count = sample_count // up_count
    cleaned = (spectra[:, 0].astype(jnp.float32) - common[:, None, :]).reshape(
        coarse_count, beam_count, up_count, frame_count
    )
    circular = (
        spectra[:, 1].astype(jnp.float32).reshape(coarse_count, beam_count, up_count, frame_count)
    )
    power = jnp.mean(cleaned * cleaned, axis=3)
    level = jnp.mean(power, axis=(0, 2)) + epsilon
    weights = mask_grid[:, None, :] / (1.0 + power / (2.0 * level[None, :, None]))
    flagged = jnp.stack([cleaned * weights[..., None], circular * weights[..., None]])
    flagged = jnp.transpose(flagged, (0, 2, 1, 3, 4)).reshape(
        2, beam_count, coarse_count * sample_count
    )
    return flagged.astype(jnp.bfloat16)


def body(voltage_real, voltage_imag, gain_real, gain_imag, channel_mask, beam_owner):
    feed_count = voltage_real.shape[3]
    sample_count = voltage_real.shape[4]
    feed_weights = beam_table(feed_count)
    column_weights = stokes_table(CYL, UP)
    calibrated = calibrate(voltage_real, voltage_imag, gain_real, gain_imag)
    formed = beamform(calibrated, feed_weights)
    turned = lax.all_to_all(formed, "grp", split_axis=4, concat_axis=1, tiled=True)
    detected = detect_block(turned, column_weights)
    stokes = detected.reshape(detected.shape[0], 2, CYL * detected.shape[3], sample_count)
    ordered = jnp.take(stokes, beam_owner[0], axis=2)
    beam_total = FEEDS_NS * CYL
    owned = lax.all_to_all(ordered, "chan", split_axis=2, concat_axis=0, tiled=True)
    owned_sums = jnp.sum(owned[:, 0], axis=1, dtype=jnp.float32)
    common = lax.psum(owned_sums, ("chan", "grp")) / beam_total
    mask_grid = channel_mask.reshape(-1, UP).astype(jnp.float32)
    flagged = soft_flag(owned, common, mask_grid)
    flattened = common.reshape(-1)
    piece_length = flattened.shape[0] // (lax.axis_size("chan") * lax.axis_size("grp"))
    position = lax.axis_index("chan") * lax.axis_size("grp") + lax.axis_index("grp")
    common_piece = lax.dynamic_slice_in_dim(flattened, position * piece_length, piece_length)
    return (flagged, common_piece)


def solution(mesh):
    in_specs = (
        P("chan", "grp", None, None, None),
        P("chan", "grp", None, None, None),
        P("chan", "grp", None, None),
        P("chan", "grp", None, None),
        P(),
        P("grp", None),
    )
    out_specs = (P(None, ("chan", "grp"), None), P(("chan", "grp")))
    return jax.shard_map(body, mesh=mesh, in_specs=in_specs, out_specs=out_specs, check_vma=False)
```

profile of v0, /device:TPU:0, one launch (start us, length us, event | category | flops | bytes accessed | tf_op | source)
XLA Modules:
  0.0 931.7 jit_solution(13042581867903100597)
XLA Ops:
  7.2 1.1 negate_convert_fusion
  8.3 1.0 fusion.31
  9.3 12.0 %copy.44 = bf16[64,1,2,256,128]{3,4,2,0,1:T(8,128)(2,1)} copy(bf16[64,1,2,256,128]{4,3,2,1,0:T(8,128)(2,1)} %param.6) | data formatting | bytes 16777216 | tf_op args[0]
  21.3 0.0 copy-start.1
  21.3 0.0 copy-start.2
  21.3 12.0 %copy.45 = bf16[64,1,2,256,128]{3,4,2,0,1:T(8,128)(2,1)} copy(bf16[64,1,2,256,128]{4,3,2,1,0:T(8,128)(2,1)} %param.7) | data formatting | bytes 16777216 | tf_op args[1]
  33.3 0.0 copy-done.1
  33.3 0.0 copy-done.2
  33.3 14.4 %fusion.14 = (bf16[64,2,1,256,128]{3,4,2,1,0:T(8,128)(2,1)}, bf16[64,2,1,256,128]{3,4,2,1,0:T(8,128)(2,1)}) fusion(bf16[64,1,2,256,128]{3,4,2,0,1:T(8,128)(2,1)} %copy.45, bf16[64,1,2,256,128]{3,4,2,0,1:T(8,128)(2,1)} %copy.44, f32[64,2,256]{2,1,0:T(2,128)S(1)} %bitcast.100, f32[64,2,256]{2,1,0:T(2,128)S(1)} %bitcast.101), kind=kLoop, calls=%fused_computation.21 | loop fusion | flops 41943040 | bytes 33816576 | tf_op jit(solution)/shard_map/stack | solution.py:49
  47.7 15.8 %fusion.9 = bf16[64,1,2,2,256,128]{4,5,3,2,0,1:T(8,128)(2,1)} fusion(bf16[64,2,1,256,128]{3,4,2,1,0:T(8,128)(2,1)} %get-tuple-element.11, bf16[64,2,1,256,128]{3,4,2,1,0:T(8,128)(2,1)} %get-tuple-element.10, bf16[1,256,2,256]{3,1,2,0:T(8,128)(2,1)S(1)} %get-tuple-element.21, bf16[1,256,2,256]{3,1,2,0:T(8,128)(2,1)S(1)} %get-tuple-element.20), kind=kOutput, calls=%fused_computation.13 | convolution fusion | flops 8632926208 | bytes 34078720 | tf_op jit(solution)/shard_map/amrn,cyprns->cypams/dot_general | solution.py:53
  63.5 41.4 %copy.47 = bf16[64,1,2,2,256,128]{5,3,2,0,1,4:T(2,128)(2,1)} copy(bf16[64,1,2,2,256,128]{4,5,3,2,0,1:T(8,128)(2,1)} %fusion.9) | data formatting | bytes 33554432 | tf_op jit(solution)/shard_map/convert_element_type | solution.py:56
  104.9 0.0 copy-start.4
  104.9 7.4 all-to-all-start
  112.3 0.0 copy-done.4
  112.4 0.6 fusion.32
  113.0 183.0 %all-to-all-done = bf16[64,1,2,2,256,128]{5,3,2,0,1,4:T(2,128)(2,1)} async-done(((bf16[64,1,2,2,256,128]{5,3,2,0,1,4:T(2,128)(2,1)}), bf16[64,1,2,2,256,128]{5,3,2,0,1,4:T(2,128)(2,1)}, u32[]{:S(2)}, u32[]{:S(2)}) %all-to-all-start) | async-done | bytes 16777248 | tf_op jit(solution)/shard_map/all_to_all | solution.py:111
  296.0 17.4 %copy.48 = bf16[64,1,2,2,256,128]{5,4,3,2,0,1:T(8,128)(2,1)} copy(bf16[64,1,2,2,256,128]{5,3,2,0,1,4:T(2,128)(2,1)} %all-to-all-done) | data formatting | bytes 33554432 | tf_op jit(solution)/shard_map/all_to_all | solution.py:111
  313.4 30.0 %copy.49 = bf16[64,4,1,2,2,64,128]{5,6,4,3,1,0,2:T(8,128)(2,1)} copy(bf16[64,4,1,2,2,64,128]{6,5,1,4,3,0,2:T(8,128)(2,1)} %bitcast.94) | data formatting | bytes 33554432 | tf_op jit(solution)/shard_map/all_to_all | solution.py:111
  343.3 40.1 %fusion.2 = f32[64,2,2,4,64,16,8]{4,5,3,2,6,1,0:T(8,128)} fusion(bf16[64,4,2,2,64,8,16,1,1]{4,6,5,3,2,1,0,8,7:T(8,128)(2,1)} %bitcast.97, f32[1,4,16,2,4,16]{5,2,3,4,1,0:T(8,128)S(1)} %get-tuple-element.19, f32[1,4,16,2,4,16]{5,2,3,4,1,0:T(8,128)S(1)} %get-tuple-element.18), kind=kOutput, calls=%fused_computation.4 | convolution fusion | flops 12884918272 | bytes 50397184 | tf_op jit(solution)/shard_map/aekrqu,cqprmfu->cpaemkf/dot_general | solution.py:66
  383.4 26.2 %add_convert_fusion = (bf16[64,1,1,4,64,16,8]{4,5,3,2,6,1,0:T(8,128)(2,1)S(1)}, bf16[64,1,1,4,64,16,8]{4,5,3,2,6,1,0:T(8,128)(2,1)}) fusion(f32[64,2,2,4,64,16,8]{4,5,3,2,6,1,0:T(8,128)} %fusion.2), kind=kLoop, calls=%fused_computation.19 | loop fusion | flops 27262976 | bytes 41943040 | tf_op jit(solution)/shard_map/convert.8
  409.7 5.9 copy.51
  415.6 12.7 %add.210 = bf16[64,1,256,128]{2,3,0,1:T(8,128)(2,1)} reshape(bf16[64,1,1,4,64,16,8]{4,3,6,5,0,2,1:T(4,128)(2,1)} %copy.51) | data formatting | bytes 8388608 | tf_op jit(solution)/shard_map/add | solution.py:72
  428.3 6.6 copy.53
  434.9 8.3 copy.52
  443.2 13.2 %mul.473 = bf16[64,1,256,128]{2,3,0,1:T(8,128)(2,1)} reshape(bf16[64,1,1,4,64,16,8]{4,3,6,5,0,2,1:T(4,128)(2,1)} %copy.52) | data formatting | bytes 8388608 | tf_op jit(solution)/shard_map/mul | solution.py:77
  456.4 6.5 copy.54
  463.0 7.6 pad_maximum_fusion
  470.6 12.0 %gather_fusion = bf16[256,64,2,128]{3,1,2,0:T(8,128)(2,1)} fusion(bf16[64,2,256,128]{3,0,2,1:T(8,128)(2,1)} %pad_maximum_fusion, s32[1024]{0:T(1024)S(1)} %pad_clamp_fusion), kind=kCustom, calls=%fused_computation | custom fusion | bytes 16778240 | tf_op jit(solution)/shard_map/jit(_take)/gather | solution.py:114
  482.6 7.6 select_bitcast_fusion
  490.2 0.0 copy-start.3
  490.2 6.8 all-to-all-start.1
  497.0 0.2 all-reduce.2.cloned.1.call-start
  497.2 0.0 copy-done.3
  497.2 0.1 convert_element_type.140
  497.3 0.1 copy.59
  497.4 182.5 %all-to-all-done.1 = bf16[64,2,256,128]{3,0,1,2:T(8,128)(2,1)} async-done(((bf16[64,2,256,128]{3,0,1,2:T(8,128)(2,1)}), bf16[64,2,256,128]{3,0,1,2:T(8,128)(2,1)}, u32[]{:S(2)}, u32[]{:S(2)}) %all-to-all-start.1) | async-done | bytes 8388640 | tf_op jit(solution)/shard_map/all_to_all | solution.py:116
  679.9 12.3 %copy.56 = bf16[8,64,2,32,128]{4,3,2,1,0:T(8,128)(2,1)} copy(bf16[8,64,2,32,128]{4,1,2,3,0:T(8,128)(2,1)} %bitcast.34) | data formatting | bytes 16777216 | tf_op jit(solution)/shard_map/all_to_all | solution.py:116
  692.2 4.6 fusion.20
  696.8 0.0 all-reduce.2.cloned.1.call-update
  696.8 11.7 %slice_convert_fusion.1 = (f32[512,1,32,128]{3,2,1,0:T(8,128)}, f32[512,1,32,128]{3,2,1,0:T(8,128)}) fusion(bf16[512,2,32,128]{3,2,1,0:T(8,128)(2,1)} %bitcast.96), kind=kLoop, calls=%fused_computation.34 | loop fusion | flops 4194304 | bytes 25165824 | tf_op jit(solution)/shard_map/convert_element_type | solution.py:88
  708.6 10.1 %copy.57 = f32[512,1,32,128]{0,3,2,1:T(8,128)} copy(f32[512,1,32,128]{3,2,1,0:T(8,128)} %get-tuple-element.12) | data formatting | bytes 16777216 | tf_op jit(solution)/shard_map/convert_element_type | solution.py:88
  718.7 10.0 %copy.61 = f32[512,1,32,128]{0,3,2,1:T(8,128)} copy(f32[512,1,32,128]{3,2,1,0:T(8,128)} %get-tuple-element.13) | data formatting | bytes 16777216 | tf_op jit(solution)/shard_map/convert_element_type | solution.py:92
  728.7 91.5 %all-reduce.2.cloned.1.call-done = f32[512,128]{1,0:T(8,128)} async-done(((f32[512,128]{1,0:T(8,128)}), f32[512,128]{1,0:T(8,128)}) %all-reduce.2.cloned.1.call-update) | async-done | bytes 262160 | tf_op jit(solution)/shard_map/psum | solution.py:118
  820.1 1.0 fusion.42
  821.1 0.1 copy.58
  821.3 0.0 copy-start
  821.3 6.8 fusion.17
  828.0 0.3 multiply_reduce_fusion
  828.4 0.3 add_divide_fusion
  828.7 0.0 copy-done
  828.7 7.1 fusion.19
  835.8 6.3 maximum_bitcast_fusion.4
  842.1 55.2 %copy.62 = bf16[2,32,512,16,8]{1,4,3,2,0:T(8,128)(2,1)} copy(bf16[2,32,512,16,8]{2,4,3,1,0:T(8,128)(2,1)} %maximum_bitcast_fusion.4) | data formatting | bytes 16777216 | tf_op jit(solution)/shard_map/convert_element_type | solution.py:101
  897.3 26.7 %copy.63 = bf16[2,32,65536]{2,1,0:T(8,128)(2,1)} copy(bf16[2,32,65536]{1,2,0:T(8,128)(2,1)} %bitcast.93) | data formatting | bytes 16777216
  924.1 0.6 dynamic_slice.3
  (9 shorter events, 0.1 us)
Async XLA Ops:
  21.3 12.0 %copy-start.1 = (f32[64,1,2,256]{3,2,1,0:T(2,128)S(1)}, f32[64,1,2,256]{3,2,1,0:T(2,128)}, u32[]{:S(2)}) copy-start(f32[64,1,2,256]{3,2,1,0:T(2,128)} %param.9) | copy-start | bytes 393220
  21.3 12.0 %copy-start.2 = (f32[64,1,2,256]{3,2,1,0:T(2,128)S(1)}, f32[64,1,2,256]{3,2,1,0:T(2,128)}, u32[]{:S(2)}) copy-start(f32[64,1,2,256]{3,2,1,0:T(2,128)} %param.8) | copy-start | bytes 393220
  104.9 7.4 copy-start.4
  104.9 191.1 %all-to-all-start = ((bf16[64,1,2,2,256,128]{5,3,2,0,1,4:T(2,128)(2,1)}), bf16[64,1,2,2,256,128]{5,3,2,0,1,4:T(2,128)(2,1)}, u32[]{:S(2)}, u32[]{:S(2)}) async-start(bf16[64,1,2,2,256,128]{5,3,2,0,1,4:T(2,128)(2,1)} %copy.47), calls=%async_computation | async-start | bytes 33554432 | tf_op jit(solution)/shard_map/all_to_all | solution.py:111
  490.2 7.0 copy-start.3
  490.2 189.7 %all-to-all-start.1 = ((bf16[64,2,256,128]{3,0,1,2:T(8,128)(2,1)}), bf16[64,2,256,128]{3,0,1,2:T(8,128)(2,1)}, u32[]{:S(2)}, u32[]{:S(2)}) async-start(bf16[64,2,256,128]{3,0,1,2:T(8,128)(2,1)} %select_bitcast_fusion), calls=%async_computation.1 | async-start | bytes 16777216 | tf_op jit(solution)/shard_map/all_to_all | solution.py:116
  497.0 323.2 %all-reduce.2.cloned.1.call-start = ((), (), s32[]{:S(2)}) async-start(), calls=%async_computation.2 | async-start | bytes 524288 | tf_op jit(solution)/shard_map/psum | solution.py:118
  821.3 7.4 copy-start
Sparse Core Ops, SparseCore 0:
  697.0 123.1 all-reduce.1
where the time goes:
time: 943 us; the launch traced here: 932 us
  waiting for transfers between devices  457 us (48%)
  local copies, waits for them, and re-layouts  293 us (31%)
  other arithmetic  96.8 us (10%)
  matrix products  55.9 us (6%)
  starting transfers between devices  14.4 us (2%)
  between operations  14.4 us (2%)
    all_to_all x1, waiting for transfers between devices, body(): lax.all_to_all(formed, 'grp', split_axis=4, concat_axis=1, tiled=True)  183 us
    all_to_all x1, waiting for transfers between devices, body(): lax.all_to_all(ordered, 'chan', split_axis=2, concat_axis=0, tiled=True)  182 us
    psum x1, waiting for transfers between devices, body(): common = lax.psum(owned_sums, ('chan', 'grp')) / beam_total  91.5 us
    convert_element_type x1, local copies, waits for them, and re-layouts, soft_flag(): return flagged.astype(jnp.bfloat16)  55.2 us
    unnamed x13, local copies, waits for them, and re-layouts  50.7 us
    all_to_all x2, local copies, waits for them, and re-layouts, body(): lax.all_to_all(formed, 'grp', split_axis=4, concat_axis=1, tiled=True)  47.3 us
    convert_element_type x1, local copies, waits for them, and re-layouts, beamform(): return formed.astype(jnp.bfloat16)  41.4 us
    dot_general x1, matrix products, detect_block(): jnp.einsum('aekrqu,cqprmfu->cpaemkf', weights, shaped, precision=lax.Prec...  40.1 us
  transfers between devices with their start and end apart: 3, of which 3 were waited for; matrix products, arithmetic and copies ran while one was open for 4% of the time, Pallas kernels for 0%

commit v1 on v0

--- a/solution.py
+++ b/solution.py
@@ -115,7 +115,7 @@
     beam_total = FEEDS_NS * CYL
     owned = lax.all_to_all(ordered, "chan", split_axis=2, concat_axis=0, tiled=True)
     owned_sums = jnp.sum(owned[:, 0], axis=1, dtype=jnp.float32)
-    common = lax.psum(owned_sums, ("chan", "grp")) / beam_total
+    common = jnp.sum(lax.all_gather(owned_sums, ("chan", "grp")), axis=0) / beam_total
     mask_grid = channel_mask.reshape(-1, UP).astype(jnp.float32)
     flagged = soft_flag(owned, common, mask_grid)
     flattened = common.reshape(-1)

time: 943 us -> 901 us (0.955)
  waiting for transfers between devices: 457 us -> 227 us
  blocking collectives: 0 us -> 190 us
    all_to_all x0 -> x1, blocking collectives: none -> 190 us  [body(): lax.all_to_all(ordered, 'chan', split_axis=2, concat_axis=0, tiled=True)]
    all_to_all x1 -> x0, waiting for transfers between devices: 182 us -> none  [body(): lax.all_to_all(ordered, 'chan', split_axis=2, concat_axis=0, tiled=True)]
    psum x1 -> x0, waiting for transfers between devices: 91.5 us -> none  [body(): common = lax.psum(owned_sums, ('chan', 'grp')) / beam_total]
    all_gather x0 -> x1, waiting for transfers between devices: none -> 43.7 us  [body(): lax.all_gather(owned_sums, ('chan', 'grp'))]
    unnamed x13 -> x11, local copies, waits for them, and re-layouts: 50.7 us -> 50.7 us
  transfers between devices with their start and end apart: 3 -> 2, of which waited for: 3 -> 2; matrix products, arithmetic and copies ran while one was open for 4% -> 4% of each run, Pallas kernels for 0% -> 0%
where the time goes in v1:
time: 901 us; the launch traced here: 889 us
  local copies, waits for them, and re-layouts  293 us (33%)
  waiting for transfers between devices  227 us (25%)
  blocking collectives  190 us (21%)
  other arithmetic  101 us (11%)
  matrix products  56 us (6%)
  between operations  14.4 us (2%)
    all_to_all x1, blocking collectives, body(): lax.all_to_all(ordered, 'chan', split_axis=2, concat_axis=0, tiled=True)  190 us
    all_to_all x1, waiting for transfers between devices, body(): lax.all_to_all(formed, 'grp', split_axis=4, concat_axis=1, tiled=True)  183 us
    convert_element_type x1, local copies, waits for them, and re-layouts, soft_flag(): return flagged.astype(jnp.bfloat16)  55.2 us
    unnamed x11, local copies, waits for them, and re-layouts  50.7 us
    all_to_all x2, local copies, waits for them, and re-layouts, body(): lax.all_to_all(formed, 'grp', split_axis=4, concat_axis=1, tiled=True)  47.8 us
    all_gather x1, waiting for transfers between devices, body(): lax.all_gather(owned_sums, ('chan', 'grp'))  43.7 us
    convert_element_type x1, local copies, waits for them, and re-layouts, beamform(): return formed.astype(jnp.bfloat16)  41.4 us
    dot_general x1, matrix products, detect_block(): jnp.einsum('aekrqu,cqprmfu->cpaemkf', weights, shaped, precision=lax.Prec...  40.1 us
  transfers between devices with their start and end apart: 2, of which 2 were waited for; matrix products, arithmetic and copies ran while one was open for 4% of the time, Pallas kernels for 0%

profile of v1, /device:TPU:0, one launch (start us, length us, event | category | flops | bytes accessed | tf_op | source)
XLA Modules:
  0.0 888.7 jit_solution(2059386099040330898)
XLA Ops:
  7.2 1.1 negate_convert_fusion
  8.3 1.0 fusion.31
  9.3 12.0 %copy.64 = bf16[64,1,2,256,128]{3,4,2,0,1:T(8,128)(2,1)} copy(bf16[64,1,2,256,128]{4,3,2,1,0:T(8,128)(2,1)} %param.6) | data formatting | bytes 16777216 | tf_op args[0]
  21.3 0.0 copy-start
  21.3 0.0 copy-start.1
  21.3 12.0 %copy.65 = bf16[64,1,2,256,128]{3,4,2,0,1:T(8,128)(2,1)} copy(bf16[64,1,2,256,128]{4,3,2,1,0:T(8,128)(2,1)} %param.7) | data formatting | bytes 16777216 | tf_op args[1]
  33.3 0.0 copy-done
  33.3 0.0 copy-done.1
  33.3 14.4 %fusion.14 = (bf16[64,2,1,256,128]{3,4,2,1,0:T(8,128)(2,1)}, bf16[64,2,1,256,128]{3,4,2,1,0:T(8,128)(2,1)}) fusion(bf16[64,1,2,256,128]{3,4,2,0,1:T(8,128)(2,1)} %copy.65, bf16[64,1,2,256,128]{3,4,2,0,1:T(8,128)(2,1)} %copy.64, f32[64,2,256]{2,1,0:T(2,128)S(1)} %bitcast.103, f32[64,2,256]{2,1,0:T(2,128)S(1)} %bitcast.104), kind=kLoop, calls=%fused_computation.21 | loop fusion | flops 41943040 | bytes 33816576 | tf_op jit(solution)/shard_map/stack | solution.py:49
  47.7 15.9 %fusion.9 = bf16[64,1,2,2,256,128]{4,5,3,2,0,1:T(8,128)(2,1)} fusion(bf16[64,2,1,256,128]{3,4,2,1,0:T(8,128)(2,1)} %get-tuple-element.13, bf16[64,2,1,256,128]{3,4,2,1,0:T(8,128)(2,1)} %get-tuple-element.12, bf16[1,256,2,256]{3,1,2,0:T(8,128)(2,1)S(1)} %get-tuple-element.23, bf16[1,256,2,256]{3,1,2,0:T(8,128)(2,1)S(1)} %get-tuple-element.22), kind=kOutput, calls=%fused_computation.13 | convolution fusion | flops 8632926208 | bytes 34078720 | tf_op jit(solution)/shard_map/amrn,cyprns->cypams/dot_general | solution.py:53
  63.6 41.4 %copy.67 = bf16[64,1,2,2,256,128]{5,3,2,0,1,4:T(2,128)(2,1)} copy(bf16[64,1,2,2,256,128]{4,5,3,2,0,1:T(8,128)(2,1)} %fusion.9) | data formatting | bytes 33554432 | tf_op jit(solution)/shard_map/convert_element_type | solution.py:56
  105.0 0.0 copy-start.3
  105.0 7.1 all-to-all-start
  112.1 0.0 all-gather.3.cloned.1.call-start
  112.2 0.0 copy-done.3
  112.3 0.6 fusion.32
  112.9 182.9 %all-to-all-done = bf16[64,1,2,2,256,128]{5,3,2,0,1,4:T(2,128)(2,1)} async-done(((bf16[64,1,2,2,256,128]{5,3,2,0,1,4:T(2,128)(2,1)}), bf16[64,1,2,2,256,128]{5,3,2,0,1,4:T(2,128)(2,1)}, u32[]{:S(2)}, u32[]{:S(2)}) %all-to-all-start) | async-done | bytes 16777248 | tf_op jit(solution)/shard_map/all_to_all | solution.py:111
  295.8 17.8 %copy.68 = bf16[64,1,2,2,256,128]{5,4,3,2,0,1:T(8,128)(2,1)} copy(bf16[64,1,2,2,256,128]{5,3,2,0,1,4:T(2,128)(2,1)} %all-to-all-done) | data formatting | bytes 33554432 | tf_op jit(solution)/shard_map/all_to_all | solution.py:111
  313.7 29.9 %copy.69 = bf16[64,4,1,2,2,64,128]{5,6,4,3,1,0,2:T(8,128)(2,1)} copy(bf16[64,4,1,2,2,64,128]{6,5,1,4,3,0,2:T(8,128)(2,1)} %bitcast.95) | data formatting | bytes 33554432 | tf_op jit(solution)/shard_map/all_to_all | solution.py:111
  343.6 40.1 %fusion.2 = f32[64,2,2,4,64,16,8]{4,5,3,2,6,1,0:T(8,128)} fusion(bf16[64,4,2,2,64,8,16,1,1]{4,6,5,3,2,1,0,8,7:T(8,128)(2,1)} %bitcast.98, f32[1,4,16,2,4,16]{5,2,3,4,1,0:T(8,128)S(1)} %get-tuple-element.21, f32[1,4,16,2,4,16]{5,2,3,4,1,0:T(8,128)S(1)} %get-tuple-element.20), kind=kOutput, calls=%fused_computation.4 | convolution fusion | flops 12884918272 | bytes 50397184 | tf_op jit(solution)/shard_map/aekrqu,cqprmfu->cpaemkf/dot_general | solution.py:66
  383.7 26.2 %add_convert_fusion = (bf16[64,1,1,4,64,16,8]{4,5,3,2,6,1,0:T(8,128)(2,1)S(1)}, bf16[64,1,1,4,64,16,8]{4,5,3,2,6,1,0:T(8,128)(2,1)}) fusion(f32[64,2,2,4,64,16,8]{4,5,3,2,6,1,0:T(8,128)} %fusion.2), kind=kLoop, calls=%fused_computation.19 | loop fusion | flops 27262976 | bytes 41943040 | tf_op jit(solution)/shard_map/convert.8
  409.9 5.9 copy.71
  415.9 12.7 %add.208 = bf16[64,1,256,128]{2,3,0,1:T(8,128)(2,1)} reshape(bf16[64,1,1,4,64,16,8]{4,3,6,5,0,2,1:T(4,128)(2,1)} %copy.71) | data formatting | bytes 8388608 | tf_op jit(solution)/shard_map/add | solution.py:72
  428.6 6.6 copy.73
  435.2 8.3 copy.72
  443.5 12.7 %mul.473 = bf16[64,1,256,128]{2,3,0,1:T(8,128)(2,1)} reshape(bf16[64,1,1,4,64,16,8]{4,3,6,5,0,2,1:T(4,128)(2,1)} %copy.72) | data formatting | bytes 8388608 | tf_op jit(solution)/shard_map/mul | solution.py:77
  456.2 6.7 copy.74
  462.9 7.6 pad_maximum_fusion
  470.6 12.0 %gather_fusion = bf16[256,64,2,128]{3,1,2,0:T(8,128)(2,1)} fusion(bf16[64,2,256,128]{3,0,2,1:T(8,128)(2,1)} %pad_maximum_fusion, s32[1024]{0:T(1024)S(1)} %pad_clamp_fusion), kind=kCustom, calls=%fused_computation | custom fusion | bytes 16778240 | tf_op jit(solution)/shard_map/jit(_take)/gather | solution.py:114
  482.6 7.6 select_bitcast_fusion
  490.2 189.6 %all_to_all.33 = bf16[64,2,256,128]{3,0,1,2:T(8,128)(2,1)} all-to-all(bf16[64,2,256,128]{3,0,1,2:T(8,128)(2,1)} %select_bitcast_fusion), channel_id=1, replica_groups=mesh['chan'=8,'grp'=4] {'chan'}, dimensions={2} | all-to-all | bytes 16777216 | tf_op jit(solution)/shard_map/all_to_all | solution.py:116
  679.8 0.0 copy-start.2
  679.8 12.3 %copy.76 = bf16[8,64,2,32,128]{4,3,2,1,0:T(8,128)(2,1)} copy(bf16[8,64,2,32,128]{4,1,2,3,0:T(8,128)(2,1)} %bitcast.99) | data formatting | bytes 16777216 | tf_op jit(solution)/shard_map/all_to_all | solution.py:116
  692.0 4.7 fusion.20
  696.7 0.0 all-gather.3.cloned.1.call-update
  696.7 0.0 copy-done.2
  696.7 0.1 convert_element_type.140
  696.9 0.1 copy.79
  697.0 11.8 %slice_convert_fusion.1 = (f32[512,1,32,128]{3,2,1,0:T(8,128)}, f32[512,1,32,128]{3,2,1,0:T(8,128)}) fusion(bf16[512,2,32,128]{3,2,1,0:T(8,128)(2,1)} %bitcast.97), kind=kLoop, calls=%fused_computation.34 | loop fusion | flops 4194304 | bytes 25165824 | tf_op jit(solution)/shard_map/convert_element_type | solution.py:88
  708.8 9.9 %copy.77 = f32[512,1,32,128]{0,3,2,1:T(8,128)} copy(f32[512,1,32,128]{3,2,1,0:T(8,128)} %get-tuple-element.14) | data formatting | bytes 16777216 | tf_op jit(solution)/shard_map/convert_element_type | solution.py:88
  718.7 10.2 %copy.81 = f32[512,1,32,128]{0,3,2,1:T(8,128)} copy(f32[512,1,32,128]{3,2,1,0:T(8,128)} %get-tuple-element.15) | data formatting | bytes 16777216 | tf_op jit(solution)/shard_map/convert_element_type | solution.py:92
  728.8 43.7 %all-gather.3.cloned.1.call-done = f32[16384,128]{1,0:T(8,128)} async-done(((f32[512,128]{1,0:T(8,128)}), f32[16384,128]{1,0:T(8,128)}) %all-gather.3.cloned.1.call-update) | async-done | bytes 8388624 | tf_op jit(solution)/shard_map/all_gather | solution.py:118
  772.6 3.8 reduce_sum.37
  776.4 0.1 copy.78
  776.5 6.6 fusion.17
  783.2 0.3 multiply_reduce_fusion
  783.5 0.3 add_divide_fusion
  783.8 9.0 %fusion.19 = (bf16[1,512,32,16,8]{1,4,3,2,0:T(8,128)(2,1)S(1)}, bf16[1,512,32,16,8]{1,4,3,2,0:T(8,128)(2,1)}) fusion(f32[512,1,32,128]{0,3,2,1:T(8,128)} %copy.77, f32[512,32,16]{0,2,1:T(8,128)S(1)} %add_divide_fusion, f32[512,16,8]{0,2,1:T(8,128)S(1)} %bitcast.102, f32[512,1,32,128]{0,3,2,1:T(8,128)} %copy.81), kind=kLoop, calls=%fused_computation.31 | loop fusion | flops 10485760 | bytes 26476544 | tf_op jit(solution)/shard_map/convert.3
  792.7 6.3 maximum_bitcast_fusion.4
  799.1 55.2 %copy.82 = bf16[2,32,512,16,8]{1,4,3,2,0:T(8,128)(2,1)} copy(bf16[2,32,512,16,8]{2,4,3,1,0:T(8,128)(2,1)} %maximum_bitcast_fusion.4) | data formatting | bytes 16777216 | tf_op jit(solution)/shard_map/convert_element_type | solution.py:101
  854.3 26.7 %copy.83 = bf16[2,32,65536]{2,1,0:T(8,128)(2,1)} copy(bf16[2,32,65536]{1,2,0:T(8,128)(2,1)} %bitcast.94) | data formatting | bytes 16777216
  881.0 0.6 dynamic_slice.3
  (10 shorter events, 0.2 us)
Async XLA Ops:
  21.3 12.0 %copy-start = (f32[64,1,2,256]{3,2,1,0:T(2,128)S(1)}, f32[64,1,2,256]{3,2,1,0:T(2,128)}, u32[]{:S(2)}) copy-start(f32[64,1,2,256]{3,2,1,0:T(2,128)} %param.9) | copy-start | bytes 393220
  21.3 12.0 %copy-start.1 = (f32[64,1,2,256]{3,2,1,0:T(2,128)S(1)}, f32[64,1,2,256]{3,2,1,0:T(2,128)}, u32[]{:S(2)}) copy-start(f32[64,1,2,256]{3,2,1,0:T(2,128)} %param.8) | copy-start | bytes 393220
  105.0 7.2 copy-start.3
  105.0 190.8 %all-to-all-start = ((bf16[64,1,2,2,256,128]{5,3,2,0,1,4:T(2,128)(2,1)}), bf16[64,1,2,2,256,128]{5,3,2,0,1,4:T(2,128)(2,1)}, u32[]{:S(2)}, u32[]{:S(2)}) async-start(bf16[64,1,2,2,256,128]{5,3,2,0,1,4:T(2,128)(2,1)} %copy.67), calls=%async_computation | async-start | bytes 33554432 | tf_op jit(solution)/shard_map/all_to_all | solution.py:111
  112.1 660.4 %all-gather.3.cloned.1.call-start = ((), (), s32[]{:S(2)}) async-start(), calls=%async_computation.2 | async-start | bytes 8650752 | tf_op jit(solution)/shard_map/all_gather | solution.py:118
  679.8 16.9 %copy-start.2 = (s32[8192]{0:T(1024)S(1)}, s32[8192]{0:T(1024)}, u32[]{:S(2)}) copy-start(s32[8192]{0:T(1024)} %param.10) | copy-start | bytes 98308
Sparse Core Ops, SparseCore 0:
  696.8 75.6 all-gather.2
